TPU v7x, 32 devices: a whole 2x2x4 slice. The times are simulated.
32 devices in a mesh: dp: 2 (over y), expert: 4 (over z), tile: 4 (over x, core).
Axes of the slice: x: 2, y: 2, z: 4, core: 2. Of those that a mesh axis runs over, the one named last changes fastest.
Arguments:
- tokens: bfloat16 [512, 4096], P(('dp', 'expert'), 'tile'), may hold values from -6 to 6
- hidden: bfloat16 [512, 2, 7168], P(('dp', 'expert'), None, 'tile'), may hold values from -6 to 6
- routes: int32 [512, 2], P(('dp', 'expert')), may hold values from 0 to 3, all different within a row; in each aligned block of 64 rows (0 to 63, 64 to 127, ...) at most 40 rows name the same one
- lengths: int32 [8], P(('dp', 'expert')), may hold values from 1 to 64, as said below
Outputs:
- hessian_in: float32 [4, 4096, 4096], P('expert', 'tile', 'dp')
- hessian_down: float32 [4, 7168, 7168], P('expert', 'tile', 'dp')
Inputs may be any that keep to these rules, and one draw needn't show every extreme that they name: `routes`: in each aligned block of 64 rows (the rows of one group) no expert is named by more than 40 rows, a bound that some block reaches. The live rows of group g are its first lengths[g] rows; the last group is full.
All inputs are finite; a program needn't handle non-finite values.
Results may differ from a plain program's by a relative error of at most 0.0003.
Values may be sent and summed in bfloat16 or wider, within the bound.
A program may use at most 128 MiB of HBM per device.

v0:
```python
import jax
import jax.numpy as jnp
from jax import lax
from jax.sharding import PartitionSpec as P


def broadcast(value, axis, source):
    kept = jnp.where(lax.axis_index(axis) == source, value, 0).astype(value.dtype)
    return lax.psum(kept, axis)


def contract(left, right):
    return lax.dot_general(
        left, right, (((0,), (0,)), ((), ())), preferred_element_type=jnp.float32
    )


def dispatch_tables(routes, live_count, experts, share_size, senders):
    token_count = routes.shape[0]
    top_count = routes.shape[1]
    flat_routes = routes.reshape(token_count * top_count)
    pair_index = jnp.arange(token_count * top_count, dtype=jnp.int32)
    pair_live = pair_index // top_count < live_count
    expert_ids = jnp.arange(experts, dtype=jnp.int32)
    onehot = ((flat_routes[:, None] == expert_ids[None, :]) & pair_live[:, None]).astype(
        jnp.float32
    )
    before = jnp.cumsum(onehot, axis=0) - onehot
    position = jnp.sum(before * onehot, axis=1).astype(jnp.int32)
    target = (
        position // share_size * (experts * share_size)
        + flat_routes * share_size
        + position % share_size
    )
    slot_total = senders * experts * share_size
    placed = (target[None, :] == jnp.arange(slot_total, dtype=jnp.int32)[:, None]) & pair_live[
        None, :
    ]
    return (placed.astype(jnp.float32), jnp.sum(onehot, axis=0))


def on_device(tokens, hidden, routes, lengths):
    experts = lax.axis_size("expert")
    senders = lax.axis_size("dp")
    tiles = lax.axis_size("tile")
    token_count = tokens.shape[0]
    top_count = routes.shape[1]
    share_size = (5 * token_count + 2 * experts * senders - 1) // (2 * experts * senders)
    placed, local_counts = dispatch_tables(routes, lengths[0], experts, share_size, senders)
    slot_total = placed.shape[0]
    by_token = jnp.sum(placed.reshape(slot_total, token_count, top_count), axis=2).astype(
        jnp.bfloat16
    )
    send_tokens = jnp.dot(by_token, tokens, preferred_element_type=jnp.float32).astype(jnp.bfloat16)
    flat_hidden = hidden.reshape(token_count * top_count, hidden.shape[2])
    send_hidden = jnp.dot(
        placed.astype(jnp.bfloat16), flat_hidden, preferred_element_type=jnp.float32
    ).astype(jnp.bfloat16)
    slot_tokens, slot_hidden = (
        lax.all_to_all(send_tokens, ("dp", "expert"), split_axis=0, concat_axis=0, tiled=True),
        lax.all_to_all(send_hidden, ("dp", "expert"), split_axis=0, concat_axis=0, tiled=True),
    )
    global_counts = lax.psum(local_counts, ("dp", "expert"))
    own_expert = lax.axis_index("expert")
    own_count = jnp.sum(
        jnp.where(jnp.arange(experts, dtype=jnp.int32) == own_expert, global_counts, 0.0)
    )
    factor = 2.0 / jnp.maximum(own_count, 1.0)
    all_tokens, all_hidden = (
        lax.all_gather(slot_tokens, "dp", axis=0, tiled=True),
        lax.all_gather(slot_hidden, "dp", axis=0, tiled=True),
    )
    width_tokens = slot_tokens.shape[1] * tiles // senders
    width_hidden = slot_hidden.shape[1] * tiles // senders
    group_index = lax.axis_index("dp")
    if senders % tiles == 0:
        source_tile = group_index * tiles // senders
        offset_tokens = group_index * width_tokens - source_tile * slot_tokens.shape[1]
        offset_hidden = group_index * width_hidden - source_tile * slot_hidden.shape[1]
        own_tokens = lax.dynamic_slice_in_dim(all_tokens, offset_tokens, width_tokens, 1)
        own_hidden = lax.dynamic_slice_in_dim(all_hidden, offset_hidden, width_hidden, 1)
        joined = jnp.concatenate([own_tokens, own_hidden], axis=1)
        arrived = broadcast(joined, "tile", source_tile)
        column_tokens = arrived[:, :width_tokens]
        column_hidden = arrived[:, width_tokens:]
    else:
        wide_tokens, wide_hidden = (
            lax.all_gather(all_tokens, "tile", axis=1, tiled=True),
            lax.all_gather(all_hidden, "tile", axis=1, tiled=True),
        )
        column_tokens = lax.dynamic_slice_in_dim(
            wide_tokens, group_index * width_tokens, width_tokens, 1
        )
        column_hidden = lax.dynamic_slice_in_dim(
            wide_hidden, group_index * width_hidden, width_hidden, 1
        )
    gram_tokens = contract(all_tokens, column_tokens)
    gram_hidden = contract(all_hidden, column_hidden)
    return ((gram_tokens * factor)[None], (gram_hidden * factor)[None])


def solution(mesh):
    placed = (
        P(("dp", "expert"), "tile"),
        P(("dp", "expert"), None, "tile"),
        P(("dp", "expert"), None),
        P(("dp", "expert")),
    )
    return jax.shard_map(
        on_device,
        mesh=mesh,
        in_specs=placed,
        out_specs=(P("expert", "tile", "dp"), P("expert", "tile", "dp")),
        check_vma=False,
    )
```

profile of v0, /device:TPU:0, one launch (start us, length us, event | category | flops | bytes accessed | tf_op | source)
XLA Modules:
  0.0 152.8 jit_solution(17547992000557333005)
XLA Ops:
  7.2 0.0 copy-start
  7.2 0.0 copy-start.2
  7.9 0.8 copy.20
  8.7 0.1 eq.43
  8.8 0.1 fusion.5
  8.9 0.2 reduce_window_sum.11
  9.1 0.2 fusion.6
  9.3 1.2 reshape.90
  10.5 0.3 convolution_convert_fusion
  10.8 1.0 all_to_all.19
  11.8 7.3 %all-to-all-start.1 = ((bf16[8,20,1792]{2,1,0:T(8,128)(2,1)}), bf16[8,20,1792]{2,1,0:T(8,128)(2,1)S(1)}, u32[]{:S(2)}, u32[]{:S(2)}) async-start(bf16[8,20,1792]{2,1,0:T(8,128)(2,1)} %all_to_all.19), calls=%async_computation.1 | async-start | bytes 1376256 | tf_op jit(solution)/shard_map/all_to_all | solution.py:61
  19.1 0.0 all-gather.6.cloned.1.call-start
  19.1 0.1 ne.82
  19.3 0.1 copy.22
  19.4 0.1 div.25
  19.5 0.1 copy.23
  19.6 0.1 rem.32
  19.8 0.1 copy.21
  19.8 0.0 copy-done.2
  19.9 18.1 %all-to-all-done.1 = bf16[8,20,1792]{2,1,0:T(8,128)(2,1)S(1)} async-done(((bf16[8,20,1792]{2,1,0:T(8,128)(2,1)}), bf16[8,20,1792]{2,1,0:T(8,128)(2,1)S(1)}, u32[]{:S(2)}, u32[]{:S(2)}) %all-to-all-start.1) | async-done | bytes 573472 | tf_op jit(solution)/shard_map/all_to_all | solution.py:61
  38.0 0.9 all_to_all.21
  38.9 0.0 all-gather.6.cloned.1.call-update
  38.9 0.0 all-gather.4.cloned.1.call-start
  39.0 0.1 convert_reduce_fusion
  39.1 0.0 copy-done
  39.1 0.3 convolution_convert_fusion.1
  39.4 0.1 all_to_all.16
  39.5 14.5 %all_to_all.24 = bf16[8,20,1024]{2,1,0:T(8,128)(2,1)S(1)} all-to-all(bf16[8,20,1024]{2,1,0:T(8,128)(2,1)S(1)} %all_to_all.16), channel_id=1, replica_groups=mesh['dp'=2,'expert'=4,'tile'=4] {'dp','expert'}, dimensions={0} | all-to-all | bytes 655360 | tf_op jit(solution)/shard_map/all_to_all | solution.py:60
  54.0 0.1 all_to_all.18
  54.1 14.2 %all_gather.12 = bf16[320,1024]{1,0:T(8,128)(2,1)} all-gather(bf16[160,1024]{1,0:T(8,128)(2,1)S(1)} %all_to_all.18), channel_id=1, replica_groups=mesh['dp'=2,'expert'=4,'tile'=4] {'dp'}, dimensions={0}, use_global_device_ids=true | all-gather | bytes 983040 | tf_op jit(solution)/shard_map/all_gather | solution.py:70
  68.3 0.0 all-gather.4.cloned.1.call-update
  68.3 0.0 all-gather.8.cloned.1.call-start
  68.3 0.0 all-gather.6.cloned.1.call-done
  68.4 0.7 all-gather.8.cloned.1.call-update
  69.0 19.6 %psum.7 = f32[4]{0:T(128)S(1)} all-reduce(f32[4]{0:T(128)S(1)} %get-tuple-element.2), channel_id=1, replica_groups=mesh['dp'=2,'expert'=4,'tile'=4] {'dp','expert'}, use_global_device_ids=true, to_apply=%region_4.5 | all-reduce | flops 4 | bytes 32 | tf_op jit(solution)/shard_map/psum | solution.py:63
  88.6 0.6 fusion.16
  89.9 0.0 copy-start.1
  89.9 3.8 %all-gather.4.cloned.1.call-done = bf16[320,4096]{1,0:T(8,128)(2,1)} async-done(((bf16[320,1024]{1,0:T(8,128)(2,1)}), bf16[320,4096]{1,0:T(8,128)(2,1)}) %all-gather.4.cloned.1.call-update) | async-done | bytes 2621456 | tf_op jit(solution)/shard_map/all_gather | solution.py:88
  93.7 7.3 %multiply_bitcast_fusion.1 = f32[1,1024,2048]{2,1,0:T(8,128)} fusion(bf16[320,1024]{1,0:T(8,128)(2,1)} %all_gather.12, f32[]{:T(128)S(6)} %div.27, bf16[320,4096]{1,0:T(8,128)(2,1)} %all-gather.4.cloned.1.call-done, s32[]{:T(128)S(6)} %select_n.54), kind=kOutput, calls=%fused_computation.1 | convolution fusion | flops 1344274432 | bytes 10354696 | tf_op jit(solution)/shard_map/dot_general | solution.py:13
  101.0 31.0 %all-gather.8.cloned.1.call-done = bf16[320,7168]{1,0:T(8,128)(2,1)} async-done(((bf16[320,1792]{1,0:T(8,128)(2,1)}), bf16[320,7168]{1,0:T(8,128)(2,1)}) %all-gather.8.cloned.1.call-update) | async-done | bytes 4587536 | tf_op jit(solution)/shard_map/all_gather | solution.py:89
  132.0 0.0 copy-done.1
  132.0 14.3 %multiply_bitcast_fusion = f32[1,1792,3584]{2,1,0:T(8,128)} fusion(bf16[320,1792]{1,0:T(8,128)(2,1)S(1)} %copy-done.1, f32[]{:T(128)S(6)} %div.27, bf16[320,7168]{1,0:T(8,128)(2,1)} %all-gather.8.cloned.1.call-done, s32[]{:T(128)S(6)} %select_n.58), kind=kOutput, calls=%fused_computation | convolution fusion | flops 4116840448 | bytes 29130760 | tf_op jit(solution)/shard_map/dot_general | solution.py:13
  (5 shorter events, 0.1 us)
Async XLA Ops:
  7.2 31.9 %copy-start = (bf16[64,1024]{1,0:T(8,128)(2,1)S(1)}, bf16[64,1024]{1,0:T(8,128)(2,1)}, u32[]{:S(2)}) copy-start(bf16[64,1024]{1,0:T(8,128)(2,1)} %param.4) | copy-start | bytes 393220
  7.2 12.6 %copy-start.2 = (s32[64,2]{0,1:T(2,128)S(1)}, s32[64,2]{0,1:T(2,128)}, u32[]{:S(2)}) copy-start(s32[64,2]{0,1:T(2,128)} %param.6) | copy-start | bytes 1540
  11.8 26.2 %all-to-all-start.1 = ((bf16[8,20,1792]{2,1,0:T(8,128)(2,1)}), bf16[8,20,1792]{2,1,0:T(8,128)(2,1)S(1)}, u32[]{:S(2)}, u32[]{:S(2)}) async-start(bf16[8,20,1792]{2,1,0:T(8,128)(2,1)} %all_to_all.19), calls=%async_computation.1 | async-start | bytes 1376256 | tf_op jit(solution)/shard_map/all_to_all | solution.py:61
  19.1 49.3 %all-gather.6.cloned.1.call-start = ((), (), s32[]{:S(2)}) async-start(), calls=%async_computation.3 | async-start | bytes 1720320 | tf_op jit(solution)/shard_map/all_gather | solution.py:71
  38.9 54.8 %all-gather.4.cloned.1.call-start = ((), (), s32[]{:S(2)}) async-start(), calls=%async_computation.2 | async-start | bytes 3276800 | tf_op jit(solution)/shard_map/all_gather | solution.py:88
  68.3 63.7 %all-gather.8.cloned.1.call-start = ((), (), s32[]{:S(2)}) async-start(), calls=%async_computation.4 | async-start | bytes 5734400 | tf_op jit(solution)/shard_map/all_gather | solution.py:89
  89.9 42.1 %copy-start.1 = (bf16[320,1792]{1,0:T(8,128)(2,1)S(1)}, bf16[320,1792]{1,0:T(8,128)(2,1)}, u32[]{:S(2)}) copy-start(bf16[320,1792]{1,0:T(8,128)(2,1)} %all-gather.6.cloned.1.call-done) | copy-start | bytes 3440644
Sparse Core Ops, SparseCore 0:
  39.0 28.0 all-gather.5
  68.7 24.9 all-gather.3
  95.3 36.6 all-gather.7
where the time goes:
time: 153 us
  waiting for transfers between devices  53.6 us (35%)
  blocking collectives  48.3 us (32%)
  matrix products  22.1 us (14%)
  between operations  15.3 us (10%)
  starting transfers between devices  7.43 us (5%)
  local copies, waits for them, and re-layouts  4.82 us (3%)
    all_gather x1, waiting for transfers between devices, on_device(): lax.all_gather(all_hidden, 'tile', axis=1, tiled=True)  31 us
    dot_general x2, matrix products, contract(): lax.dot_general(left, right, (((0,), (0,)), ((), ())), preferred_element_...  21.6 us
    psum x1, blocking collectives, on_device(): global_counts = lax.psum(local_counts, ('dp', 'expert'))  19.6 us
    all_to_all x1, waiting for transfers between devices, on_device(): lax.all_to_all(send_hidden, ('dp', 'expert'), split_axis=0, concat_axis=0...  18.1 us
    all_to_all x1, blocking collectives, on_device(): lax.all_to_all(send_tokens, ('dp', 'expert'), split_axis=0, concat_axis=0...  14.5 us
    all_gather x1, blocking collectives, on_device(): lax.all_gather(slot_tokens, 'dp', axis=0, tiled=True)  14.2 us
    all_to_all x1, starting transfers between devices, on_device(): lax.all_to_all(send_hidden, ('dp', 'expert'), split_axis=0, concat_axis=0...  7.31 us
    all_gather x1, waiting for transfers between devices, on_device(): lax.all_gather(all_tokens, 'tile', axis=1, tiled=True)  3.79 us
  transfers between devices with their start and end apart: 4, of which 3 were waited for; matrix products, arithmetic and copies ran while one was open for 6% of the time, Pallas kernels for 0%

commit v1 on v0

--- a/solution.py
+++ b/solution.py
@@ -1,7 +1,14 @@
+import functools
+
 import jax
 import jax.numpy as jnp
 from jax import lax
+from jax.experimental import pallas as pl
+from jax.experimental.pallas import tpu as pltpu
 from jax.sharding import PartitionSpec as P
+
+MESH = pl.DeviceIdType.MESH
+ROW_BLOCK = 256
 
 
 def broadcast(value, axis, source):
@@ -39,7 +46,7 @@
     return (placed.astype(jnp.float32), jnp.sum(onehot, axis=0))
 
 
-def on_device(tokens, hidden, routes, lengths):
+def general(tokens, hidden, routes, lengths):
     experts = lax.axis_size("expert")
     senders = lax.axis_size("dp")
     tiles = lax.axis_size("tile")
@@ -99,6 +106,266 @@
     return ((gram_tokens * factor)[None], (gram_hidden * factor)[None])
 
 
+def packed_rows(tokens, hidden, routes, live_count, experts, cap):
+    token_count, top_count = routes.shape
+    flat_routes = routes.reshape(token_count * top_count)
+    pair_index = jnp.arange(token_count * top_count, dtype=jnp.int32)
+    pair_live = pair_index // top_count < live_count
+    expert_ids = jnp.arange(experts, dtype=jnp.int32)
+    onehot = ((flat_routes[:, None] == expert_ids[None, :]) & pair_live[:, None]).astype(
+        jnp.float32
+    )
+    earlier = (pair_index[None, :] < pair_index[:, None]).astype(jnp.float32)
+    before = jnp.dot(earlier, onehot)
+    position = jnp.sum(before * onehot, axis=1).astype(jnp.int32)
+    target = jnp.where(pair_live, flat_routes * cap + position, -1)
+    placed = (target[None, :] == jnp.arange(experts * cap, dtype=jnp.int32)[:, None]).astype(
+        jnp.bfloat16
+    )
+    by_token = jnp.sum(placed.reshape(experts * cap, token_count, top_count), axis=2)
+    send_tokens = jnp.dot(by_token, tokens, preferred_element_type=jnp.float32)
+    flat_hidden = hidden.reshape(token_count * top_count, hidden.shape[2])
+    send_hidden = jnp.dot(placed, flat_hidden, preferred_element_type=jnp.float32)
+    packed = jnp.concatenate(
+        [send_tokens.astype(jnp.bfloat16), send_hidden.astype(jnp.bfloat16)], axis=1
+    )
+    return packed.reshape(experts, cap, packed.shape[1]), jnp.sum(onehot, axis=0)
+
+
+def exchange(experts, own_ref, count_ref, all_ref, counts_ref, local_sem, send_sem, recv_sem,
+             count_send, count_recv):
+    d, e, t = lax.axis_index("dp"), lax.axis_index("expert"), lax.axis_index("tile")
+    x, c = t // 2, t % 2
+    other = 1 - d
+    unequal = (x + d) % 2
+    own_slot = (1 - unequal) * c + unequal * 2
+    along_y = {"dp": other, "expert": e, "tile": t}
+    along_x = {"dp": d, "expert": e, "tile": t + 2 - 4 * x}
+    sibling = {"dp": d, "expert": e, "tile": t + 1 - 2 * c}
+    peers = [{"dp": d, "expert": (e + k) % experts, "tile": t} for k in range(1, experts)]
+    far = [{"dp": other, "expert": (e + k) % experts, "tile": t} for k in range(experts)]
+
+    barrier = pltpu.get_barrier_semaphore()
+    greeted = peers + far + [along_x, sibling]
+    for peer in greeted:
+        pl.semaphore_signal(barrier, inc=1, device_id=peer, device_id_type=MESH)
+    pl.semaphore_wait(barrier, len(greeted))
+
+    def send(source, slot, group, z, peer, kind, k):
+        copy = pltpu.make_async_remote_copy(
+            src_ref=source,
+            dst_ref=all_ref.at[slot, group, z],
+            send_sem=send_sem.at[kind, k],
+            recv_sem=recv_sem.at[slot, group, z],
+            device_id=peer,
+            device_id_type=MESH,
+        )
+        copy.start()
+        return copy
+
+    def arrived(slot, group, z):
+        pltpu.make_async_copy(
+            all_ref.at[slot, group, z], all_ref.at[slot, group, z], recv_sem.at[slot, group, z]
+        ).wait()
+
+    first = [
+        send(own_ref.at[(e + k) % experts], own_slot, d, e, peers[k - 1], 0, k)
+        for k in range(1, experts)
+    ]
+    local = pltpu.make_async_copy(own_ref.at[e], all_ref.at[own_slot, d, e], local_sem.at[0])
+    local.start()
+    zs = [(e + experts - k) % experts for k in range(experts)]
+
+    def source(slot, k):
+        return own_ref.at[e] if k == 0 else all_ref.at[slot, d, zs[k]]
+
+    @pl.when(unequal == 0)
+    def _():
+        started = []
+
+        def relay(k):
+            z = zs[k]
+            arrived(c, other, z)
+            held = all_ref.at[c, other, z]
+            if k % 2 == 0:
+                started.append(send(held, c, other, z, along_x, 5, k))
+            started.append(send(held, c, other, z, sibling, 4, k))
+            if k % 2 == 1:
+                arrived(2, d, z)
+                started.append(send(all_ref.at[2, d, z], c, d, z, along_y, 5, k))
+
+        for k in range(experts):
+            if k:
+                arrived(c, d, zs[k])
+            started.append(send(source(c, k), c, d, zs[k], along_x, 2, k))
+            started.append(send(source(c, k), 2, d, zs[k], along_y, 1, k))
+            started.append(send(source(c, k), c, d, zs[k], sibling, 3, k))
+            if k:
+                relay(k - 1)
+        relay(experts - 1)
+        for k in range(experts):
+            arrived(1 - c, d, zs[k])
+            arrived(1 - c, other, zs[k])
+        for copy in started:
+            copy.wait_send()
+
+    @pl.when(unequal == 1)
+    def _():
+        started = []
+
+        def share(group, k, kind):
+            arrived(c, group, zs[k])
+            started.append(
+                send(all_ref.at[c, group, zs[k]], c, group, zs[k], sibling, kind, k)
+            )
+
+        for k in range(experts):
+            if k:
+                arrived(2, d, zs[k])
+            started.append(send(source(2, k), c, d, zs[k], along_y, 1, k))
+            if k % 2 == 1:
+                started.append(send(source(2, k), 2, d, zs[k], along_x, 2, k))
+            if k >= 1:
+                share(d, k - 1, 3)
+            if k >= 2:
+                share(other, k - 2, 4)
+        share(d, experts - 1, 3)
+        for k in range(max(experts - 2, 0), experts):
+            share(other, k, 4)
+        for k in range(experts):
+            arrived(2, other, zs[k])
+            arrived(1 - c, d, zs[k])
+            arrived(1 - c, other, zs[k])
+        for copy in started:
+            copy.wait_send()
+
+    told = []
+    for index, peer in enumerate(peers + far):
+        copy = pltpu.make_async_remote_copy(
+            src_ref=count_ref.at[peer["expert"]],
+            dst_ref=counts_ref.at[d, e],
+            send_sem=count_send.at[index],
+            recv_sem=count_recv.at[d, e],
+            device_id=peer,
+            device_id_type=MESH,
+        )
+        copy.start()
+        told.append(copy)
+    own_count = pltpu.make_async_copy(count_ref.at[e], counts_ref.at[d, e], local_sem.at[1])
+    own_count.start()
+    for peer in peers + far:
+        pltpu.make_async_copy(
+            counts_ref.at[peer["dp"], peer["expert"]],
+            counts_ref.at[peer["dp"], peer["expert"]],
+            count_recv.at[peer["dp"], peer["expert"]],
+        ).wait()
+    for copy in told + first:
+        copy.wait_send()
+    own_count.wait()
+    local.wait()
+
+
+def grams(steps_down, width_in, sel_ref, left_ref, columns_ref, counts_ref, in_ref, down_ref):
+    step = pl.program_id(0)
+    total = jnp.sum(counts_ref[...], axis=0)[0:1, 0:1]
+    factor = 2.0 / jnp.maximum(total, 1.0)
+    left = left_ref[0]
+
+    def fill(out_ref, start, width):
+        for k in range(2):
+            for at in range(0, width, width // 2):
+                out_ref[0, :, k * width + at : k * width + at + width // 2] = (
+                    contract(
+                        left, columns_ref[k, :, start + at : start + at + width // 2]
+                    )
+                    * factor
+                )
+
+    @pl.when(step < steps_down)
+    def _():
+        fill(down_ref, width_in, columns_ref.shape[2] - width_in)
+
+    @pl.when(step >= steps_down)
+    def _():
+        fill(in_ref, 0, width_in)
+
+
+def direct(tokens, hidden, routes, lengths, cap):
+    experts = lax.axis_size("expert")
+    width_in, width_down = tokens.shape[1], hidden.shape[2]
+    features = width_in + width_down
+    packed, local_counts = packed_rows(tokens, hidden, routes, lengths[0], experts, cap)
+    count_tiles = jnp.broadcast_to(local_counts[:, None, None], (experts, 8, 128))
+    gathered, counts = pl.pallas_call(
+        functools.partial(exchange, experts),
+        out_shape=(
+            jax.ShapeDtypeStruct((3, 2, experts, cap, features), jnp.bfloat16),
+            jax.ShapeDtypeStruct((2, experts, 8, 128), jnp.float32),
+        ),
+        in_specs=[pl.BlockSpec(memory_space=pltpu.VMEM)] * 2,
+        out_specs=[pl.BlockSpec(memory_space=pl.ANY)] * 2,
+        scratch_shapes=[
+            pltpu.SemaphoreType.DMA((2,)),
+            pltpu.SemaphoreType.DMA((6, experts)),
+            pltpu.SemaphoreType.DMA((3, 2, experts)),
+            pltpu.SemaphoreType.DMA((2 * experts - 1,)),
+            pltpu.SemaphoreType.DMA((2, experts)),
+        ],
+        compiler_params=pltpu.CompilerParams(collective_id=0, has_side_effects=True),
+        name="exchange",
+    )(packed, count_tiles)
+    rows = 2 * experts * cap
+    tile, group = lax.axis_index("tile"), lax.axis_index("dp")
+    left_slot = jnp.where(tile // 2 == group, tile % 2, 2).astype(jnp.int32).reshape(1)
+    steps_in, steps_down = width_in // ROW_BLOCK, width_down // ROW_BLOCK
+    steps = steps_in + steps_down
+    joined = gathered.reshape(3, rows, features)
+    return pl.pallas_call(
+        functools.partial(grams, steps_down, width_in),
+        out_shape=(
+            jax.ShapeDtypeStruct((1, width_in, 2 * width_in), jnp.float32),
+            jax.ShapeDtypeStruct((1, width_down, 2 * width_down), jnp.float32),
+        ),
+        grid_spec=pltpu.PrefetchScalarGridSpec(
+            num_scalar_prefetch=1,
+            grid=(steps,),
+            in_specs=[
+                pl.BlockSpec(
+                    (1, rows, ROW_BLOCK), lambda i, sel: (sel[0], 0, (i + steps_in) % steps)
+                ),
+                pl.BlockSpec((2, rows, features), lambda i, sel: (0, 0, 0)),
+                pl.BlockSpec((2 * experts, 8, 128), lambda i, sel: (0, 0, 0)),
+            ],
+            out_specs=(
+                pl.BlockSpec(
+                    (1, ROW_BLOCK, 2 * width_in),
+                    lambda i, sel: (0, jnp.maximum(i - steps_down, 0), 0),
+                ),
+                pl.BlockSpec(
+                    (1, ROW_BLOCK, 2 * width_down),
+                    lambda i, sel: (0, jnp.minimum(i, steps_down - 1), 0),
+                ),
+            ),
+        ),
+        compiler_params=pltpu.CompilerParams(
+            dimension_semantics=("arbitrary",), vmem_limit_bytes=48 * 1024 * 1024
+        ),
+        name="grams",
+    )(left_slot, joined, joined, counts.reshape(2 * experts, 8, 128))
+
+
+def on_device(tokens, hidden, routes, lengths):
+    experts = lax.axis_size("expert")
+    senders = lax.axis_size("dp")
+    token_count = tokens.shape[0]
+    share_size = (5 * token_count + 2 * experts * senders - 1) // (2 * experts * senders)
+    cap = share_size * senders
+    fits = tokens.shape[1] % ROW_BLOCK == 0 and hidden.shape[2] % ROW_BLOCK == 0
+    if senders == 2 and lax.axis_size("tile") == 4 and cap % 8 == 0 and fits:
+        return direct(tokens, hidden, routes, lengths, cap)
+    return general(tokens, hidden, routes, lengths)
+
+
 def solution(mesh):
     placed = (
         P(("dp", "expert"), "tile"),

time: 153 us -> 82.4 us (0.54)
  Pallas kernels: 0 us -> 71.8 us
  waiting for transfers between devices: 53.6 us -> 0 us
  blocking collectives: 48.3 us -> 0 us
  matrix products: 22.1 us -> 0.71 us
  between operations: 15.3 us -> 1.43 us
  starting transfers between devices: 7.43 us -> 0 us
    pallas_call x0 -> x2, Pallas kernels: none -> 71.8 us  [the longest x1 55.1 us: direct(): pl.pallas_call(functools.partial(exchange, experts), out_shape=(jax.Shape...]
    all_gather x3 -> x0, waiting for transfers between devices: 34.8 us -> none  [the longest x1 31 us: on_device(): lax.all_gather(all_hidden, 'tile', axis=1, tiled=True)]
    dot_general x4 -> x3, matrix products: 22.1 us -> 0.71 us  [the longest x1 0.3 us: packed_rows(): jnp.dot(placed, flat_hidden, preferred_element_type=jnp.float32)]
    psum x1 -> x0, blocking collectives: 19.6 us -> none  [on_device(): global_counts = lax.psum(local_counts, ('dp', 'expert'))]
    all_to_all x1 -> x0, waiting for transfers between devices: 18.1 us -> none  [on_device(): lax.all_to_all(send_hidden, ('dp', 'expert'), split_axis=0, concat_axis=0...]
    all_to_all x1 -> x0, blocking collectives: 14.5 us -> none  [on_device(): lax.all_to_all(send_tokens, ('dp', 'expert'), split_axis=0, concat_axis=0...]
    all_gather x1 -> x0, blocking collectives: 14.2 us -> none  [on_device(): lax.all_gather(slot_tokens, 'dp', axis=0, tiled=True)]
    all_to_all x1 -> x0, starting transfers between devices: 7.31 us -> none  [on_device(): lax.all_to_all(send_hidden, ('dp', 'expert'), split_axis=0, concat_axis=0...]
  transfers between devices with their start and end apart: 4 -> 0, of which waited for: 3 -> 0; matrix products, arithmetic and copies ran while one was open for 6% -> 0% of each run, Pallas kernels for 0% -> 0%
where the time goes in v1:
time: 82.4 us; the launch traced here: 82.1 us
  Pallas kernels  71.8 us (87%)
  local copies, waits for them, and re-layouts  6.27 us (8%)
  other arithmetic  1.92 us (2%)
  between operations  1.43 us (2%)
    pallas_call x1, Pallas kernels, direct(): pl.pallas_call(functools.partial(exchange, experts), out_shape=(jax.Shape...  55.1 us
    pallas_call x1, Pallas kernels, direct(): pl.pallas_call(functools.partial(grams, steps_down, width_in), out_shape=...  16.7 us
    unnamed x7, local copies, waits for them, and re-layouts  4.06 us

profile of v1, /device:TPU:0, one launch (start us, length us, event | category | flops | bytes accessed | tf_op | source)
XLA Modules:
  0.0 82.1 jit_solution(1700397486573532252)
XLA Ops:
  0.6 0.0 copy-start
  1.4 0.8 copy.16
  2.1 0.1 eq.41
  2.3 0.1 fusion
  2.4 0.1 convert_reduce_fusion
  2.6 0.7 broadcast_in_dim.3.count_ref
  3.3 0.1 convert_element_type.28
  3.4 0.1 copy.17
  3.5 0.7 compare_select_fusion
  4.2 0.1 fusion.2
  4.3 0.0 copy-done
  4.3 0.3 convolution_convert_fusion.1
  4.5 1.2 %reshape.75 = bf16[128,1792]{1,0:T(8,128)(2,1)S(1)} reshape(bf16[64,2,1792]{2,1,0:T(2,128)(2,1)} %param.5) | data formatting | bytes 917504 | tf_op jit(solution)/shard_map/reshape | solution.py:127
  5.7 0.3 convolution_convert_fusion
  6.0 1.0 %pad_maximum_fusion = bf16[160,2816]{1,0:T(8,128)(2,1)} fusion(bf16[160,1792]{1,0:T(8,128)(2,1)S(1)} %convolution_convert_fusion, bf16[160,1024]{1,0:T(8,128)(2,1)S(1)} %convolution_convert_fusion.1), kind=kLoop, calls=%fused_computation.4 | loop fusion | flops 1802240 | bytes 1802240 | tf_op jit(solution)/shard_map/concatenate | solution.py:129
  7.0 55.1 %exchange.1 = (bf16[3,2,4,40,2816]{4,3,2,1,0:T(8,128)(2,1)}, f32[2,4,8,128]{3,2,1,0:T(8,128)}) custom-call(bf16[4,40,2816]{2,1,0:T(8,128)(2,1)} %bitcast.14, f32[4,8,128]{2,1,0:T(8,128)} %broadcast_in_dim.3.count_ref), custom_call_target="tpu_custom_call" | custom-call | tf_op jit(solution)/shard_map/exchange/pallas_call | solution.py:299
  62.1 0.0 copy-start.1
  62.1 2.5 %copy-done.1 = bf16[3,2,4,40,2816]{4,3,2,1,0:T(8,128)(2,1)S(1)} copy-done((bf16[3,2,4,40,2816]{4,3,2,1,0:T(8,128)(2,1)S(1)}, bf16[3,2,4,40,2816]{4,3,2,1,0:T(8,128)(2,1)}, u32[]{:S(2)}) %copy-start.1) | copy-done | bytes 5406744
  64.6 0.0 copy-start.2
  64.7 0.8 copy-done.2
  65.4 16.7 %grams.1 = (f32[1,1024,2048]{2,1,0:T(8,128)}, f32[1,1792,3584]{2,1,0:T(8,128)}) custom-call(s32[1]{0:T(128)} %bitcast.sel_ref, bf16[3,320,2816]{2,1,0:T(8,128)(2,1)S(1)} %bitcast.11, bf16[3,320,2816]{2,1,0:T(8,128)(2,1)S(1)} %bitcast.12, f32[8,8,128]{2,1,0:T(8,128)S(1)} %bitcast.13), custom_call_target="tpu_custom_call" | custom-call | tf_op jit(solution)/shard_map/grams/pallas_call | solution.py:323
  (3 shorter events, 0.0 us)
Async XLA Ops:
  0.6 3.6 %copy-start = (bf16[64,1024]{1,0:T(8,128)(2,1)S(1)}, bf16[64,1024]{1,0:T(8,128)(2,1)}, u32[]{:S(2)}) copy-start(bf16[64,1024]{1,0:T(8,128)(2,1)} %param.4) | copy-start | bytes 393220
  62.1 2.5 %copy-start.1 = (bf16[3,2,4,40,2816]{4,3,2,1,0:T(8,128)(2,1)S(1)}, bf16[3,2,4,40,2816]{4,3,2,1,0:T(8,128)(2,1)}, u32[]{:S(2)}) copy-start(bf16[3,2,4,40,2816]{4,3,2,1,0:T(8,128)(2,1)} %get-tuple-element.4) | copy-start | bytes 16220164
  64.6 0.8 copy-start.2

commit v2 on v1

--- a/solution.py
+++ b/solution.py
@@ -106,30 +106,49 @@
     return ((gram_tokens * factor)[None], (gram_hidden * factor)[None])
 
 
-def packed_rows(tokens, hidden, routes, live_count, experts, cap):
-    token_count, top_count = routes.shape
-    flat_routes = routes.reshape(token_count * top_count)
-    pair_index = jnp.arange(token_count * top_count, dtype=jnp.int32)
-    pair_live = pair_index // top_count < live_count
-    expert_ids = jnp.arange(experts, dtype=jnp.int32)
-    onehot = ((flat_routes[:, None] == expert_ids[None, :]) & pair_live[:, None]).astype(
-        jnp.float32
-    )
-    earlier = (pair_index[None, :] < pair_index[:, None]).astype(jnp.float32)
-    before = jnp.dot(earlier, onehot)
-    position = jnp.sum(before * onehot, axis=1).astype(jnp.int32)
-    target = jnp.where(pair_live, flat_routes * cap + position, -1)
-    placed = (target[None, :] == jnp.arange(experts * cap, dtype=jnp.int32)[:, None]).astype(
-        jnp.bfloat16
-    )
-    by_token = jnp.sum(placed.reshape(experts * cap, token_count, top_count), axis=2)
-    send_tokens = jnp.dot(by_token, tokens, preferred_element_type=jnp.float32)
-    flat_hidden = hidden.reshape(token_count * top_count, hidden.shape[2])
-    send_hidden = jnp.dot(placed, flat_hidden, preferred_element_type=jnp.float32)
-    packed = jnp.concatenate(
-        [send_tokens.astype(jnp.bfloat16), send_hidden.astype(jnp.bfloat16)], axis=1
-    )
-    return packed.reshape(experts, cap, packed.shape[1]), jnp.sum(onehot, axis=0)
+def pack(experts, cap, live_ref, routes_ref, tokens_ref, hidden_ref, packed_ref, count_ref):
+    token_count, width_in = tokens_ref.shape
+    routes = routes_ref[...]
+    row = lax.broadcasted_iota(jnp.int32, (1, token_count), 1)
+    live = row < live_ref[0]
+    first, second = routes[0:1], routes[1:2]
+    expert_ids = lax.broadcasted_iota(jnp.int32, (experts, token_count), 0)
+    hits = jnp.where(((first == expert_ids) | (second == expert_ids)) & live, 1.0, 0.0)
+    earlier = jnp.where(
+        lax.broadcasted_iota(jnp.int32, (token_count, token_count), 0)
+        < lax.broadcasted_iota(jnp.int32, (token_count, token_count), 1),
+        1.0,
+        0.0,
+    )
+    before = jnp.dot(
+        hits.astype(jnp.bfloat16), earlier.astype(jnp.bfloat16), preferred_element_type=jnp.float32
+    )
+    slot = lax.broadcasted_iota(jnp.int32, (cap, token_count), 0).astype(jnp.float32)
+    by_first, by_second = [], []
+    for expert in range(experts):
+        hit = hits[expert : expert + 1]
+        placed = jnp.where(slot == before[expert : expert + 1], hit, 0.0)
+        by_first.append(jnp.where(first == expert, placed, 0.0))
+        by_second.append(jnp.where(second == expert, placed, 0.0))
+        total = jnp.sum(hit, axis=1, keepdims=True)
+        count_ref[expert] = jnp.broadcast_to(total, count_ref.shape[1:])
+    by_first = jnp.concatenate(by_first, axis=0)
+    by_second = jnp.concatenate(by_second, axis=0)
+    by_token = (by_first + by_second).astype(jnp.bfloat16)
+    by_first, by_second = by_first.astype(jnp.bfloat16), by_second.astype(jnp.bfloat16)
+
+    def put(rows, start):
+        for expert in range(experts):
+            packed_ref[expert, :, start : start + rows.shape[1]] = rows[
+                expert * cap : (expert + 1) * cap
+            ].astype(jnp.bfloat16)
+
+    put(jnp.dot(by_token, tokens_ref[...], preferred_element_type=jnp.float32), 0)
+    put(
+        jnp.dot(by_first, hidden_ref[:, 0, :], preferred_element_type=jnp.float32)
+        + jnp.dot(by_second, hidden_ref[:, 1, :], preferred_element_type=jnp.float32),
+        width_in,
+    )
 
 
 def exchange(experts, own_ref, count_ref, all_ref, counts_ref, local_sem, send_sem, recv_sem,
@@ -168,13 +187,47 @@
             all_ref.at[slot, group, z], all_ref.at[slot, group, z], recv_sem.at[slot, group, z]
         ).wait()
 
+    low = e // 2
+    zs = [e, 1 - e + 4 * low, 2 - low, 3 - 3 * low]
+    middle = (e + low) % 2
+
     first = [
-        send(own_ref.at[(e + k) % experts], own_slot, d, e, peers[k - 1], 0, k)
+        pltpu.make_async_remote_copy(
+            src_ref=own_ref.at[zs[k]],
+            dst_ref=all_ref.at[own_slot, d, e],
+            send_sem=send_sem.at[0, k],
+            recv_sem=recv_sem.at[own_slot, d, e],
+            device_id={"dp": d, "expert": zs[k], "tile": t},
+            device_id_type=MESH,
+        )
         for k in range(1, experts)
     ]
+    first[0].start()
+
+    @pl.when(middle == 1)
+    def _():
+        first[1].start()
+
     local = pltpu.make_async_copy(own_ref.at[e], all_ref.at[own_slot, d, e], local_sem.at[0])
     local.start()
-    zs = [(e + experts - k) % experts for k in range(experts)]
+
+    def second_sends():
+        first[0].wait_send()
+
+        @pl.when(middle == 0)
+        def _():
+            first[1].start()
+
+        @pl.when(middle == 1)
+        def _():
+            first[1].wait_send()
+            first[2].start()
+
+    def third_sends():
+        @pl.when(middle == 0)
+        def _():
+            first[1].wait_send()
+            first[2].start()
 
     def source(slot, k):
         return own_ref.at[e] if k == 0 else all_ref.at[slot, d, zs[k]]
@@ -200,9 +253,11 @@
             started.append(send(source(c, k), c, d, zs[k], along_x, 2, k))
             started.append(send(source(c, k), 2, d, zs[k], along_y, 1, k))
             started.append(send(source(c, k), c, d, zs[k], sibling, 3, k))
-            if k:
-                relay(k - 1)
-        relay(experts - 1)
+            if k == 0:
+                second_sends()
+            relay(k)
+            if k == 1:
+                third_sends()
         for k in range(experts):
             arrived(1 - c, d, zs[k])
             arrived(1 - c, other, zs[k])
@@ -225,13 +280,14 @@
             started.append(send(source(2, k), c, d, zs[k], along_y, 1, k))
             if k % 2 == 1:
                 started.append(send(source(2, k), 2, d, zs[k], along_x, 2, k))
+            if k == 0:
+                second_sends()
             if k >= 1:
-                share(d, k - 1, 3)
-            if k >= 2:
-                share(other, k - 2, 4)
-        share(d, experts - 1, 3)
-        for k in range(max(experts - 2, 0), experts):
-            share(other, k, 4)
+                share(other, k - 1, 4)
+            if k == 1:
+                third_sends()
+            share(d, k, 3)
+        share(other, experts - 1, 4)
         for k in range(experts):
             arrived(2, other, zs[k])
             arrived(1 - c, d, zs[k])
@@ -259,7 +315,7 @@
             counts_ref.at[peer["dp"], peer["expert"]],
             count_recv.at[peer["dp"], peer["expert"]],
         ).wait()
-    for copy in told + first:
+    for copy in told + first[2:]:
         copy.wait_send()
     own_count.wait()
     local.wait()
@@ -294,15 +350,24 @@
     experts = lax.axis_size("expert")
     width_in, width_down = tokens.shape[1], hidden.shape[2]
     features = width_in + width_down
-    packed, local_counts = packed_rows(tokens, hidden, routes, lengths[0], experts, cap)
-    count_tiles = jnp.broadcast_to(local_counts[:, None, None], (experts, 8, 128))
+    vmem = pl.BlockSpec(memory_space=pltpu.VMEM)
+    packed, count_tiles = pl.pallas_call(
+        functools.partial(pack, experts, cap),
+        out_shape=(
+            jax.ShapeDtypeStruct((experts, cap, features), jnp.bfloat16),
+            jax.ShapeDtypeStruct((experts, 8, 128), jnp.float32),
+        ),
+        in_specs=[pl.BlockSpec(memory_space=pltpu.SMEM), vmem, vmem, vmem],
+        out_specs=[vmem, vmem],
+        name="pack",
+    )(lengths, routes.T, tokens, hidden)
     gathered, counts = pl.pallas_call(
         functools.partial(exchange, experts),
         out_shape=(
             jax.ShapeDtypeStruct((3, 2, experts, cap, features), jnp.bfloat16),
             jax.ShapeDtypeStruct((2, experts, 8, 128), jnp.float32),
         ),
-        in_specs=[pl.BlockSpec(memory_space=pltpu.VMEM)] * 2,
+        in_specs=[vmem, vmem],
         out_specs=[pl.BlockSpec(memory_space=pl.ANY)] * 2,
         scratch_shapes=[
             pltpu.SemaphoreType.DMA((2,)),
@@ -348,7 +413,7 @@
             ),
         ),
         compiler_params=pltpu.CompilerParams(
-            dimension_semantics=("arbitrary",), vmem_limit_bytes=48 * 1024 * 1024
+            dimension_semantics=("arbitrary",), vmem_limit_bytes=66_000_000
         ),
         name="grams",
     )(left_slot, joined, joined, counts.reshape(2 * experts, 8, 128))
@@ -361,7 +426,8 @@
     share_size = (5 * token_count + 2 * experts * senders - 1) // (2 * experts * senders)
     cap = share_size * senders
     fits = tokens.shape[1] % ROW_BLOCK == 0 and hidden.shape[2] % ROW_BLOCK == 0
-    if senders == 2 and lax.axis_size("tile") == 4 and cap % 8 == 0 and fits:
+    square = senders == 2 and experts == 4 and lax.axis_size("tile") == 4 and routes.shape[1] == 2
+    if square and cap % 8 == 0 and fits:
         return direct(tokens, hidden, routes, lengths, cap)
     return general(tokens, hidden, routes, lengths)
 

time: 82.4 us -> 76.6 us (0.930)
  local copies, waits for them, and re-layouts: 6.27 us -> 0 us
  Pallas kernels: 71.8 us -> 75.1 us
  other arithmetic: 1.92 us -> 0 us
    unnamed x7 -> x0, local copies, waits for them, and re-layouts: 4.06 us -> none
    pallas_call x0 -> x1, Pallas kernels: none -> 3.36 us  [direct(): pl.pallas_call(functools.partial(pack, experts, cap), out_shape=(jax.Shap...]
    pallas_call x1, Pallas kernels: 55.1 us -> 52.7 us  [direct(): pl.pallas_call(functools.partial(exchange, experts), out_shape=(jax.Shape...]
    pallas_call x1, Pallas kernels: 16.7 us -> 19.1 us  [direct(): pl.pallas_call(functools.partial(grams, steps_down, width_in), out_shape=...]
    reshape x1 -> x0, local copies, waits for them, and re-layouts: 1.19 us -> none  [packed_rows(): flat_hidden = hidden.reshape(token_count * top_count, hidden.shape[2])]
    concatenate x1 -> x0, other arithmetic: 0.98 us -> none  [packed_rows(): jnp.concatenate([send_tokens.astype(jnp.bfloat16), send_hidden.astype(jnp...]
where the time goes in v2:
time: 76.6 us; the launch traced here: 76.4 us
  Pallas kernels  75.1 us (98%)
  between operations  1.31 us (2%)
    pallas_call x1, Pallas kernels, direct(): pl.pallas_call(functools.partial(exchange, experts), out_shape=(jax.Shape...  52.7 us
    pallas_call x1, Pallas kernels, direct(): pl.pallas_call(functools.partial(grams, steps_down, width_in), out_shape=...  19.1 us
    pallas_call x1, Pallas kernels, direct(): pl.pallas_call(functools.partial(pack, experts, cap), out_shape=(jax.Shap...  3.36 us

profile of v2, /device:TPU:0, one launch (start us, length us, event | category | flops | bytes accessed | tf_op | source)
XLA Modules:
  0.0 76.4 jit_solution(2402610919924698410)
XLA Ops:
  1.3 3.4 %pack.1 = (bf16[4,40,2816]{2,1,0:T(8,128)(2,1)}, f32[4,8,128]{2,1,0:T(8,128)}) custom-call(s32[1]{0:T(128)S(6)} %copy.6.live_ref, s32[2,64]{1,0:T(2,128)} %bitcast.7, bf16[64,1024]{1,0:T(8,128)(2,1)} %tokens_ref.1, bf16[64,2,1792]{2,1,0:T(2,128)(2,1)} %hidden_ref.1), custom_call_target="tpu_custom_call" | custom-call | tf_op jit(solution)/shard_map/pack/pallas_call | solution.py:354
  4.7 52.7 %exchange.1 = (bf16[3,2,4,40,2816]{4,3,2,1,0:T(8,128)(2,1)}, f32[2,4,8,128]{3,2,1,0:T(8,128)}) custom-call(bf16[4,40,2816]{2,1,0:T(8,128)(2,1)} %get-tuple-element.6.own_ref, f32[4,8,128]{2,1,0:T(8,128)} %get-tuple-element.7.count_ref), custom_call_target="tpu_custom_call" | custom-call | tf_op jit(solution)/shard_map/exchange/pallas_call | solution.py:364
  57.4 19.1 %grams.1 = (f32[1,1024,2048]{2,1,0:T(8,128)}, f32[1,1792,3584]{2,1,0:T(8,128)}) custom-call(s32[1]{0:T(128)} %bitcast.sel_ref, bf16[3,320,2816]{2,1,0:T(8,128)(2,1)} %bitcast.4, bf16[3,320,2816]{2,1,0:T(8,128)(2,1)} %bitcast.5, f32[8,8,128]{2,1,0:T(8,128)} %bitcast.6), custom_call_target="tpu_custom_call" | custom-call | tf_op jit(solution)/shard_map/grams/pallas_call | solution.py:388

commit v3 on v2

--- a/solution.py
+++ b/solution.py
@@ -9,6 +9,7 @@
 
 MESH = pl.DeviceIdType.MESH
 ROW_BLOCK = 256
+PIECES = 2
 
 
 def broadcast(value, axis, source):
@@ -170,130 +171,145 @@
         pl.semaphore_signal(barrier, inc=1, device_id=peer, device_id_type=MESH)
     pl.semaphore_wait(barrier, len(greeted))
 
-    def send(source, slot, group, z, peer, kind, k):
+    width = all_ref.shape[4] // PIECES
+    spans = [pl.ds(piece * width, width) for piece in range(PIECES)]
+
+    def send(source, slot, group, z, peer, kind, k, piece):
         copy = pltpu.make_async_remote_copy(
-            src_ref=source,
-            dst_ref=all_ref.at[slot, group, z],
-            send_sem=send_sem.at[kind, k],
-            recv_sem=recv_sem.at[slot, group, z],
+            src_ref=source.at[:, spans[piece]],
+            dst_ref=all_ref.at[slot, group, z, :, spans[piece]],
+            send_sem=send_sem.at[kind, k, piece],
+            recv_sem=recv_sem.at[slot, group, z, piece],
             device_id=peer,
             device_id_type=MESH,
         )
         copy.start()
         return copy
 
-    def arrived(slot, group, z):
-        pltpu.make_async_copy(
-            all_ref.at[slot, group, z], all_ref.at[slot, group, z], recv_sem.at[slot, group, z]
-        ).wait()
+    def arrived(slot, group, z, piece):
+        here = all_ref.at[slot, group, z, :, spans[piece]]
+        pltpu.make_async_copy(here, here, recv_sem.at[slot, group, z, piece]).wait()
 
     low = e // 2
     zs = [e, 1 - e + 4 * low, 2 - low, 3 - 3 * low]
     middle = (e + low) % 2
 
     first = [
-        pltpu.make_async_remote_copy(
-            src_ref=own_ref.at[zs[k]],
-            dst_ref=all_ref.at[own_slot, d, e],
-            send_sem=send_sem.at[0, k],
-            recv_sem=recv_sem.at[own_slot, d, e],
-            device_id={"dp": d, "expert": zs[k], "tile": t},
-            device_id_type=MESH,
-        )
+        [
+            pltpu.make_async_remote_copy(
+                src_ref=own_ref.at[zs[k], :, span],
+                dst_ref=all_ref.at[own_slot, d, e, :, span],
+                send_sem=send_sem.at[0, k, piece],
+                recv_sem=recv_sem.at[own_slot, d, e, piece],
+                device_id={"dp": d, "expert": zs[k], "tile": t},
+                device_id_type=MESH,
+            )
+            for piece, span in enumerate(spans)
+        ]
         for k in range(1, experts)
     ]
-    first[0].start()
+
+    def start(copies):
+        for copy in copies:
+            copy.start()
+
+    def left(copies):
+        for copy in copies:
+            copy.wait_send()
+
+    start(first[0])
 
     @pl.when(middle == 1)
     def _():
-        first[1].start()
+        start(first[1])
 
     local = pltpu.make_async_copy(own_ref.at[e], all_ref.at[own_slot, d, e], local_sem.at[0])
     local.start()
 
     def second_sends():
-        first[0].wait_send()
+        left(first[0])
 
         @pl.when(middle == 0)
         def _():
-            first[1].start()
+            start(first[1])
 
         @pl.when(middle == 1)
         def _():
-            first[1].wait_send()
-            first[2].start()
+            left(first[1])
+            start(first[2])
 
     def third_sends():
         @pl.when(middle == 0)
         def _():
-            first[1].wait_send()
-            first[2].start()
+            left(first[1])
+            start(first[2])
 
     def source(slot, k):
         return own_ref.at[e] if k == 0 else all_ref.at[slot, d, zs[k]]
+
+    pieces = [(k, piece) for k in range(experts) for piece in range(PIECES)]
 
     @pl.when(unequal == 0)
     def _():
         started = []
 
-        def relay(k):
+        def relay(k, piece):
             z = zs[k]
-            arrived(c, other, z)
+            arrived(c, other, z, piece)
             held = all_ref.at[c, other, z]
             if k % 2 == 0:
-                started.append(send(held, c, other, z, along_x, 5, k))
-            started.append(send(held, c, other, z, sibling, 4, k))
+                started.append(send(held, c, other, z, along_x, 5, k, piece))
+            started.append(send(held, c, other, z, sibling, 4, k, piece))
             if k % 2 == 1:
-                arrived(2, d, z)
-                started.append(send(all_ref.at[2, d, z], c, d, z, along_y, 5, k))
+                arrived(2, d, z, piece)
+                started.append(send(all_ref.at[2, d, z], c, d, z, along_y, 5, k, piece))
 
         for k in range(experts):
-            if k:
-                arrived(c, d, zs[k])
-            started.append(send(source(c, k), c, d, zs[k], along_x, 2, k))
-            started.append(send(source(c, k), 2, d, zs[k], along_y, 1, k))
-            started.append(send(source(c, k), c, d, zs[k], sibling, 3, k))
+            for piece in range(PIECES):
+                if k:
+                    arrived(c, d, zs[k], piece)
+                started.append(send(source(c, k), c, d, zs[k], along_x, 2, k, piece))
+                started.append(send(source(c, k), 2, d, zs[k], along_y, 1, k, piece))
+                started.append(send(source(c, k), c, d, zs[k], sibling, 3, k, piece))
             if k == 0:
                 second_sends()
-            relay(k)
+            for piece in range(PIECES):
+                relay(k, piece)
             if k == 1:
                 third_sends()
-        for k in range(experts):
-            arrived(1 - c, d, zs[k])
-            arrived(1 - c, other, zs[k])
-        for copy in started:
-            copy.wait_send()
+        for k, piece in pieces:
+            arrived(1 - c, d, zs[k], piece)
+            arrived(1 - c, other, zs[k], piece)
+        left(started)
 
     @pl.when(unequal == 1)
     def _():
         started = []
 
-        def share(group, k, kind):
-            arrived(c, group, zs[k])
-            started.append(
-                send(all_ref.at[c, group, zs[k]], c, group, zs[k], sibling, kind, k)
-            )
+        def share(group, k, kind, piece):
+            arrived(c, group, zs[k], piece)
+            held = all_ref.at[c, group, zs[k]]
+            started.append(send(held, c, group, zs[k], sibling, kind, k, piece))
 
         for k in range(experts):
-            if k:
-                arrived(2, d, zs[k])
-            started.append(send(source(2, k), c, d, zs[k], along_y, 1, k))
-            if k % 2 == 1:
-                started.append(send(source(2, k), 2, d, zs[k], along_x, 2, k))
+            for piece in range(PIECES):
+                if k:
+                    arrived(2, d, zs[k], piece)
+                started.append(send(source(2, k), c, d, zs[k], along_y, 1, k, piece))
+                if k % 2 == 1:
+                    started.append(send(source(2, k), 2, d, zs[k], along_x, 2, k, piece))
             if k == 0:
                 second_sends()
-            if k >= 1:
-                share(other, k - 1, 4)
             if k == 1:
                 third_sends()
-            share(d, k, 3)
-        share(other, experts - 1, 4)
-        for k in range(experts):
-            arrived(2, other, zs[k])
-            arrived(1 - c, d, zs[k])
-            arrived(1 - c, other, zs[k])
-        for copy in started:
-            copy.wait_send()
+        for k, piece in pieces:
+            share(d, k, 3, piece)
+            share(other, k, 4, piece)
+        for k, piece in pieces:
+            arrived(2, other, zs[k], piece)
+            arrived(1 - c, d, zs[k], piece)
+            arrived(1 - c, other, zs[k], piece)
+        left(started)
 
     told = []
     for index, peer in enumerate(peers + far):
@@ -315,8 +331,7 @@
             counts_ref.at[peer["dp"], peer["expert"]],
             count_recv.at[peer["dp"], peer["expert"]],
         ).wait()
-    for copy in told + first[2:]:
-        copy.wait_send()
+    left(told + first[2])
     own_count.wait()
     local.wait()
 
@@ -371,8 +386,8 @@
         out_specs=[pl.BlockSpec(memory_space=pl.ANY)] * 2,
         scratch_shapes=[
             pltpu.SemaphoreType.DMA((2,)),
-            pltpu.SemaphoreType.DMA((6, experts)),
-            pltpu.SemaphoreType.DMA((3, 2, experts)),
+            pltpu.SemaphoreType.DMA((6, experts, PIECES)),
+            pltpu.SemaphoreType.DMA((3, 2, experts, PIECES)),
             pltpu.SemaphoreType.DMA((2 * experts - 1,)),
             pltpu.SemaphoreType.DMA((2, experts)),
         ],

time: 76.6 us -> 74 us (0.966)
  Pallas kernels: 75.1 us -> 72.5 us
    pallas_call x1, Pallas kernels: 52.7 us -> 50.1 us  [direct(): pl.pallas_call(functools.partial(exchange, experts), out_shape=(jax.Shape...]
where the time goes in v3:
time: 74 us; the launch traced here: 73.8 us
  Pallas kernels  72.5 us (98%)
  between operations  1.31 us (2%)
    pallas_call x1, Pallas kernels, direct(): pl.pallas_call(functools.partial(exchange, experts), out_shape=(jax.Shape...  50.1 us
    pallas_call x1, Pallas kernels, direct(): pl.pallas_call(functools.partial(grams, steps_down, width_in), out_shape=...  19.1 us
    pallas_call x1, Pallas kernels, direct(): pl.pallas_call(functools.partial(pack, experts, cap), out_shape=(jax.Shap...  3.36 us

profile of v3, /device:TPU:0, one launch (start us, length us, event | category | flops | bytes accessed | tf_op | source)
XLA Modules:
  0.0 73.8 jit_solution(13432721955206244757)
XLA Ops:
  1.3 3.4 %pack.1 = (bf16[4,40,2816]{2,1,0:T(8,128)(2,1)}, f32[4,8,128]{2,1,0:T(8,128)}) custom-call(s32[1]{0:T(128)S(6)} %copy.6.live_ref, s32[2,64]{1,0:T(2,128)} %bitcast.7, bf16[64,1024]{1,0:T(8,128)(2,1)} %tokens_ref.1, bf16[64,2,1792]{2,1,0:T(2,128)(2,1)} %hidden_ref.1), custom_call_target="tpu_custom_call" | custom-call | tf_op jit(solution)/shard_map/pack/pallas_call | solution.py:369
  4.7 50.1 %exchange.1 = (bf16[3,2,4,40,2816]{4,3,2,1,0:T(8,128)(2,1)}, f32[2,4,8,128]{3,2,1,0:T(8,128)}) custom-call(bf16[4,40,2816]{2,1,0:T(8,128)(2,1)} %get-tuple-element.6.own_ref, f32[4,8,128]{2,1,0:T(8,128)} %get-tuple-element.7.count_ref), custom_call_target="tpu_custom_call" | custom-call | tf_op jit(solution)/shard_map/exchange/pallas_call | solution.py:379
  54.7 19.1 %grams.1 = (f32[1,1024,2048]{2,1,0:T(8,128)}, f32[1,1792,3584]{2,1,0:T(8,128)}) custom-call(s32[1]{0:T(128)} %bitcast.sel_ref, bf16[3,320,2816]{2,1,0:T(8,128)(2,1)} %bitcast.4, bf16[3,320,2816]{2,1,0:T(8,128)(2,1)} %bitcast.5, f32[8,8,128]{2,1,0:T(8,128)} %bitcast.6), custom_call_target="tpu_custom_call" | custom-call | tf_op jit(solution)/shard_map/grams/pallas_call | solution.py:403
